TPU v7x, 512 devices: a whole 4x8x8 slice. The times are simulated.
512 devices in a mesh: row: 16 (over x, z_lo), col: 32 (over y, z_hi, core).
Axes of the slice: x: 4, y: 8, z: 8 (z_hi: 2, z_lo: 4; z = z_hi * 4 + z_lo), core: 2. Of those that a mesh axis runs over, the one named last changes fastest.
Arguments:
- amplitudes: float32 [32, 96, 4, 128, 128], P('col', 'row'), may hold values from -6 to 6
- integrals: float32 [2, 2048, 16384], P(None, 'row', 'col'), may hold values from -0.25 to 0.25
- owner_column: int32 [2], replicated, may hold values from 0 to 31
- occ_irrep: int32 [96], replicated, may hold values from 0 to 7, as said below
- pair_irrep: int32 [2, 16], replicated, may hold values from 0 to 7, as said below
Outputs:
- ladder: float32 [12288, 16384], P('row', 'col')
Inputs may be any that keep to these rules, and one draw needn't show every extreme that they name: `occ_irrep`: every irrep 0 to 7 labels some occupied-pair tile. `pair_irrep`: in each section no irrep labels more than 4 of the 16 panel tiles, and some irrep labels exactly 4.
All inputs are finite; a program needn't handle non-finite values.
Results may differ from a plain program's by a relative error of at most 0.0001.
Values sent between devices are 32-bit elements; how exact they have to be, the bound alone decides.
A program may use at most 64 MiB of HBM per device.

v0:
```python
import jax
import jax.numpy as jnp
from jax import lax
from jax.sharding import PartitionSpec as P


def spread(value, axis, source):
    kept = jnp.where(lax.axis_index(axis) == source, value, 0).astype(value.dtype)
    return lax.psum(kept, axis)


def slot_tables(occ_labels, pair_labels, slot_count):
    matches = occ_labels[:, None] == pair_labels[None, :]
    order_rank = jnp.cumsum(matches.astype(jnp.int32), axis=1) - 1
    slot_ids = jnp.arange(slot_count, dtype=jnp.int32)
    chosen = matches[:, None, :] & (order_rank[:, None, :] == slot_ids[None, :, None])
    positions = jnp.arange(pair_labels.shape[0], dtype=jnp.int32)
    tile_index = jnp.sum(chosen.astype(jnp.int32) * positions[None, None, :], axis=2)
    valid_slot = jnp.any(chosen, axis=2)
    return (tile_index, valid_slot, chosen)


def on_device(amplitudes, integrals, owner_column, occ_irrep, pair_irrep):
    tiles_here = amplitudes.shape[1]
    slot_count = amplitudes.shape[2]
    tile_size = amplitudes.shape[3]
    section_count = integrals.shape[0]
    columns = integrals.shape[2]
    first_tile = lax.axis_index("row") * tiles_here
    occ_mine = lax.dynamic_slice_in_dim(occ_irrep, first_tile, tiles_here)

    def fetch_panel(which_section):
        return spread(amplitudes[0], "col", owner_column[which_section])

    tables = [
        slot_tables(occ_mine, pair_irrep[which_section], slot_count)
        for which_section in range(section_count)
    ]
    panels = [fetch_panel(which_section) for which_section in range(section_count)]
    section_rows = [
        lax.all_gather(integrals[which_section], "row", axis=0, tiled=True)
        for which_section in range(section_count)
    ]
    running = jnp.zeros((tiles_here, tile_size, columns), jnp.float32)
    for which_section in range(section_count):
        tile_index, valid_slot, chosen = tables[which_section]
        amp_panel = panels[which_section] * valid_slot[:, :, None, None].astype(jnp.float32)
        row_tiles = section_rows[which_section].reshape(-1, tile_size, columns)
        picked = jnp.take(row_tiles, tile_index, axis=0)
        running = running + jnp.einsum(
            "osij,osjv->oiv", amp_panel, picked, precision=lax.Precision.HIGHEST
        )
    return running.reshape(tiles_here * tile_size, columns)


def solution(mesh):
    return jax.shard_map(
        on_device,
        mesh=mesh,
        in_specs=(P("col", "row", None, None, None), P(None, "row", "col"), P(), P(), P()),
        out_specs=P("row", "col"),
        check_vma=False,
    )
```

profile of v0, /device:TPU:1, one launch (start us, length us, event | category | flops | bytes accessed | tf_op | source)
XLA Modules:
  0.0 477.0 jit_solution(14299060480379461248)
XLA Ops:
  7.4 0.0 copy-start.3
  7.4 0.0 copy-start.1
  7.4 0.0 all-gather.7.cloned.1.call-start
  7.4 2.0 fusion.24
  9.4 0.0 all-gather.7.cloned.1.call-update
  9.4 0.0 all-gather.5.cloned.1.call-start
  9.4 0.7 all-gather.5.cloned.1.call-update
  10.2 0.0 all-reduce.3.cloned.1.call-start
  10.2 0.0 copy-done.3
  10.2 0.6 fusion.25
  12.2 0.0 copy-done.1
  12.2 2.0 select_bitcast_fusion.1
  14.2 0.0 copy-start.5
  14.2 0.0 copy-start.4
  14.2 0.0 all-reduce.3.cloned.1.call-update
  14.3 0.6 copy-done.5
  14.9 0.1 dynamic_slice.3
  15.0 0.0 copy-done.4
  15.0 0.1 broadcast_compare_fusion.1
  15.1 0.2 reduce_window_sum.18
  15.2 0.2 select_reduce_fusion
  15.4 0.1 reshape.163
  15.5 0.2 fusion.18
  15.7 0.2 reduce_window_sum.17
  15.9 0.2 select_reduce_fusion.1
  16.1 0.1 reshape.159
  16.1 0.2 fusion.19
  16.4 133.2 %all-gather.7.cloned.1.call-done = f32[1,2048,512]{2,1,0:T(8,128)} async-done(((f32[1,128,512]{2,1,0:T(8,128)}), f32[1,2048,512]{2,1,0:T(8,128)}) %all-gather.7.cloned.1.call-update) | async-done | bytes 4194320 | tf_op jit(solution)/shard_map/all_gather | solution.py:41
  149.6 5.8 %gather_fusion.1 = f32[24,128,512]{2,1,0:T(8,128)} fusion(f32[16,128,512]{2,1,0:T(8,128)} %bitcast.23, s32[1024]{0:T(1024)S(1)} %pad_clamp_fusion), kind=kCustom, calls=%fused_computation.1.clone | custom fusion | bytes 12583008 | tf_op jit(solution)/shard_map/jit(_take)/gather | solution.py:49
  155.4 130.0 %all-gather.5.cloned.1.call-done = f32[1,2048,512]{2,1,0:T(8,128)} async-done(((f32[1,128,512]{2,1,0:T(8,128)}), f32[1,2048,512]{2,1,0:T(8,128)}) %all-gather.5.cloned.1.call-update) | async-done | bytes 4194320 | tf_op jit(solution)/shard_map/all_gather | solution.py:41
  285.4 5.8 %gather_fusion = f32[24,128,512]{2,1,0:T(8,128)} fusion(f32[16,128,512]{2,1,0:T(8,128)} %bitcast.24, s32[1024]{0:T(1024)S(1)} %pad_clamp_fusion.1), kind=kCustom, calls=%fused_computation.clone | custom fusion | bytes 12583008 | tf_op jit(solution)/shard_map/jit(_take)/gather | solution.py:49
  291.2 166.4 %all-reduce.3.cloned.1.call-done = (f32[6,4,128,128]{3,2,1,0:T(8,128)}, f32[6,4,128,128]{3,2,1,0:T(8,128)}) async-done(((f32[6,4,128,128]{3,2,1,0:T(8,128)}, f32[6,4,128,128]{3,2,1,0:T(8,128)}), (f32[6,4,128,128]{3,2,1,0:T(8,128)}, f32[6,4,128,128]{3,2,1,0:T(8,128)})) %all-reduce.3.cloned.1.call-update) | async-done | bytes 3145744 | tf_op jit(solution)/shard_map/psum | solution.py:9
  457.6 0.0 copy-start
  457.6 0.0 copy-start.2
  457.6 6.9 %fusion = f32[6,128,512,1]{2,1,3,0:T(8,128)S(1)} fusion(f32[6,4,128,512]{3,2,1,0:T(8,128)} %bitcast.21, pred[6,4]{1,0:T(8,128)(4,1)S(1)} %compare_and_fusion, f32[6,4,128,128]{3,2,1,0:T(8,128)} %get-tuple-element.6, f32[6,4]{1,0:T(8,128)S(1)} %convert_element_type.38), kind=kOutput, calls=%fused_computation.2 | convolution fusion | flops 2417885184 | bytes 9437304 | tf_op jit(solution)/shard_map/osij,osjv->oiv/dot_general | solution.py:50
  464.6 0.0 copy-done
  464.6 0.0 copy-done.2
  464.6 5.0 %bitcast_add_fusion = f32[6,128,512]{2,1,0:T(8,128)} fusion(f32[6,128,512,1]{2,1,3,0:T(8,128)S(1)} %fusion, f32[6,4,128,512]{3,2,1,0:T(8,128)S(1)} %bitcast.22, pred[6,4]{1,0:T(8,128)(4,1)S(1)} %compare_and_fusion.1, f32[6,4,128,128]{3,2,1,0:T(8,128)S(1)} %copy-done.2, f32[6,4]{1,0:T(8,128)S(1)} %convert_element_type.36), kind=kOutput, calls=%fused_computation.10 | convolution fusion | flops 2418278400 | bytes 11010168 | tf_op jit(solution)/shard_map/osij,osjv->oiv/dot_general | solution.py:50
  (11 shorter events, 0.1 us)
Async XLA Ops:
  7.4 2.8 copy-start.3
  7.4 4.8 %copy-start.1 = (f32[1,6,4,128,128]{4,3,2,1,0:T(8,128)S(1)}, f32[1,6,4,128,128]{4,3,2,1,0:T(8,128)}, u32[]{:S(2)}) copy-start(f32[1,6,4,128,128]{4,3,2,1,0:T(8,128)} %param.7) | copy-start | bytes 4718596
  7.4 142.2 %all-gather.7.cloned.1.call-start = ((), (), s32[]{:S(2)}) async-start(), calls=%async_computation.1 | async-start | bytes 4456448 | tf_op jit(solution)/shard_map/all_gather | solution.py:41
  9.4 276.0 %all-gather.5.cloned.1.call-start = ((), (), s32[]{:S(2)}) async-start(), calls=%async_computation | async-start | bytes 4456448 | tf_op jit(solution)/shard_map/all_gather | solution.py:41
  10.2 447.5 %all-reduce.3.cloned.1.call-start = ((), (), s32[]{:S(2)}) async-start(), calls=%async_computation.2 | async-start | bytes 6291456 | tf_op jit(solution)/shard_map/psum | solution.py:9
  14.2 0.7 copy-start.5
  14.2 0.7 copy-start.4
  457.6 7.0 %copy-start = (f32[24,128,512]{2,1,0:T(8,128)S(1)}, f32[24,128,512]{2,1,0:T(8,128)}, u32[]{:S(2)}) copy-start(f32[24,128,512]{2,1,0:T(8,128)} %gather_fusion) | copy-start | bytes 18874372
  457.6 7.0 %copy-start.2 = (f32[6,4,128,128]{3,2,1,0:T(8,128)S(1)}, f32[6,4,128,128]{3,2,1,0:T(8,128)}, u32[]{:S(2)}) copy-start(f32[6,4,128,128]{3,2,1,0:T(8,128)} %get-tuple-element.7) | copy-start | bytes 4718596
Sparse Core Ops, SparseCore 0:
  10.3 139.2 all-gather.6
  151.9 133.4 all-gather.4
Sparse Core Ops, SparseCore 1:
  14.4 443.2 all-reduce.2
where the time goes:
time: 477 us
  waiting for transfers between devices  430 us (90%)
  between operations  16.3 us (3%)
  local copies, waits for them, and re-layouts  15.1 us (3%)
  matrix products  12 us (3%)
    all_gather x2, waiting for transfers between devices, on_device(): lax.all_gather(integrals[which_section], 'row', axis=0, tiled=True)  263 us
    psum x1, waiting for transfers between devices, spread(): return lax.psum(kept, axis)  166 us
    dot_general x2, matrix products, on_device(): jnp.einsum('osij,osjv->oiv', amp_panel, picked, precision=lax.Precision.H...  12 us
    gather x2, local copies, waits for them, and re-layouts, on_device(): picked = jnp.take(row_tiles, tile_index, axis=0)  11.6 us
  transfers between devices with their start and end apart: 3, of which 3 were waited for; matrix products, arithmetic and copies ran while one was open for 3% of the time, Pallas kernels for 0%

commit v1 on v0

--- a/solution.py
+++ b/solution.py
@@ -38,7 +38,12 @@
     ]
     panels = [fetch_panel(which_section) for which_section in range(section_count)]
     section_rows = [
-        lax.all_gather(integrals[which_section], "row", axis=0, tiled=True)
+        jnp.concatenate(
+            lax.all_to_all(
+                jnp.stack([integrals[which_section]] * lax.axis_size("row")), "row", 0, 0
+            ),
+            axis=0,
+        )
         for which_section in range(section_count)
     ]
     running = jnp.zeros((tiles_here, tile_size, columns), jnp.float32)

time: 477 us -> 552 us (1.16)
  blocking collectives: 0 us -> 105 us
  waiting for transfers between devices: 430 us -> 393 us
    all_gather x2 -> x0, waiting for transfers between devices: 263 us -> none  [on_device(): lax.all_gather(integrals[which_section], 'row', axis=0, tiled=True)]
    psum x1, waiting for transfers between devices: 166 us -> 393 us  [spread(): return lax.psum(kept, axis)]
    all_to_all x0 -> x1, blocking collectives: none -> 105 us  [on_device(): lax.all_to_all(jnp.stack([integrals[which_section]] * lax.axis_size('row'...]
  transfers between devices with their start and end apart: 3 -> 2, of which waited for: 3 -> 1; matrix products, arithmetic and copies ran while one was open for 3% -> 3% of each run, Pallas kernels for 0% -> 0%
where the time goes in v1:
time: 552 us; the launch traced here: 551 us
  waiting for transfers between devices  393 us (71%)
  blocking collectives  105 us (19%)
  local copies, waits for them, and re-layouts  17.4 us (3%)
  between operations  14.9 us (3%)
  matrix products  13.7 us (2%)
    psum x1, waiting for transfers between devices, spread(): return lax.psum(kept, axis)  393 us
    all_to_all x1, blocking collectives, on_device(): lax.all_to_all(jnp.stack([integrals[which_section]] * lax.axis_size('row'...  105 us
    dot_general x2, matrix products, on_device(): jnp.einsum('osij,osjv->oiv', amp_panel, picked, precision=lax.Precision.H...  13.7 us
    gather x2, local copies, waits for them, and re-layouts, on_device(): picked = jnp.take(row_tiles, tile_index, axis=0)  11.7 us
  transfers between devices with their start and end apart: 2, of which 1 were waited for; matrix products, arithmetic and copies ran while one was open for 3% of the time, Pallas kernels for 0%

profile of v1, /device:TPU:1, one launch (start us, length us, event | category | flops | bytes accessed | tf_op | source)
XLA Modules:
  0.0 551.4 jit_solution(6765733735056756164)
XLA Ops:
  6.5 1.1 slice_bitcast_fusion.1
  7.6 0.5 stack.7
  8.1 104.6 %all_to_all.10 = f32[16,128,512]{2,1,0:T(8,128)} all-to-all(f32[16,128,512]{2,1,0:T(8,128)S(1)} %stack.7), channel_id=1, replica_groups=mesh['row'=16,'col'=32] {'row'}, dimensions={0} | all-to-all | bytes 8388608 | tf_op jit(solution)/shard_map/all_to_all | solution.py:42
  112.8 2.6 stack.6
  115.4 0.0 copy-start.2
  115.4 0.0 copy-start
  115.4 4.7 all-to-all-start
  120.1 0.0 all-reduce.3.cloned.1.call-start
  120.1 0.0 copy-done.2
  120.1 0.7 fusion.24
  122.2 0.0 copy-done
  122.2 2.1 select_bitcast_fusion.1
  124.3 0.0 copy-start.4
  124.3 0.0 copy-start.3
  124.3 0.0 all-reduce.3.cloned.1.call-update
  124.3 0.6 copy-done.4
  124.9 0.1 dynamic_slice.3
  125.0 0.0 copy-done.3
  125.0 0.1 broadcast_compare_fusion.1
  125.1 0.2 reduce_window_sum.18
  125.2 0.2 select_reduce_fusion
  125.4 0.1 reshape.153
  125.5 0.2 fusion.18
  125.7 0.2 reduce_window_sum.17
  125.9 0.2 select_reduce_fusion.1
  126.1 0.1 reshape.149
  126.2 0.2 fusion.19
  126.4 5.8 %gather_fusion.1 = f32[24,128,512]{2,1,0:T(8,128)} fusion(f32[16,128,512]{2,1,0:T(8,128)} %all_to_all.10, s32[1024]{0:T(1024)S(1)} %pad_clamp_fusion), kind=kCustom, calls=%fused_computation.1.clone | custom fusion | bytes 12583008 | tf_op jit(solution)/shard_map/jit(_take)/gather | solution.py:54
  132.2 392.7 %all-reduce.3.cloned.1.call-done = (f32[6,4,128,128]{3,2,1,0:T(8,128)}, f32[6,4,128,128]{3,2,1,0:T(8,128)}) async-done(((f32[6,4,128,128]{3,2,1,0:T(8,128)}, f32[6,4,128,128]{3,2,1,0:T(8,128)}), (f32[6,4,128,128]{3,2,1,0:T(8,128)}, f32[6,4,128,128]{3,2,1,0:T(8,128)})) %all-reduce.3.cloned.1.call-update) | async-done | bytes 3145744 | tf_op jit(solution)/shard_map/psum | solution.py:9
  525.0 6.8 %fusion = f32[6,128,512,1]{2,1,3,0:T(8,128)S(1)} fusion(f32[6,4,128,512]{3,2,1,0:T(8,128)} %bitcast.23, pred[6,4]{1,0:T(8,128)(4,1)S(1)} %compare_and_fusion, f32[6,4,128,128]{3,2,1,0:T(8,128)} %get-tuple-element.6, f32[6,4]{1,0:T(8,128)S(1)} %convert_element_type.38), kind=kOutput, calls=%fused_computation.2 | convolution fusion | flops 2417885184 | bytes 9437304 | tf_op jit(solution)/shard_map/osij,osjv->oiv/dot_general | solution.py:55
  531.8 0.0 copy-start.1
  531.8 0.0 all-to-all-done
  531.8 5.9 %gather_fusion = f32[24,128,512]{2,1,0:T(8,128)} fusion(f32[16,128,512]{2,1,0:T(8,128)} %all-to-all-done, s32[1024]{0:T(1024)S(1)} %pad_clamp_fusion.1), kind=kCustom, calls=%fused_computation.clone | custom fusion | bytes 12583008 | tf_op jit(solution)/shard_map/jit(_take)/gather | solution.py:54
  537.7 0.0 copy-done.1
  537.7 6.9 %bitcast_add_fusion = f32[6,128,512]{2,1,0:T(8,128)} fusion(f32[6,128,512,1]{2,1,3,0:T(8,128)S(1)} %fusion, f32[6,4,128,512]{3,2,1,0:T(8,128)} %bitcast.24, pred[6,4]{1,0:T(8,128)(4,1)S(1)} %compare_and_fusion.1, f32[6,4,128,128]{3,2,1,0:T(8,128)S(1)} %copy-done.1, f32[6,4]{1,0:T(8,128)S(1)} %convert_element_type.36), kind=kOutput, calls=%fused_computation.10 | convolution fusion | flops 2418278400 | bytes 11010168 | tf_op jit(solution)/shard_map/osij,osjv->oiv/dot_general | solution.py:55
  (11 shorter events, 0.1 us)
Async XLA Ops:
  115.4 4.7 copy-start.2
  115.4 6.8 %copy-start = (f32[1,6,4,128,128]{4,3,2,1,0:T(8,128)S(1)}, f32[1,6,4,128,128]{4,3,2,1,0:T(8,128)}, u32[]{:S(2)}) copy-start(f32[1,6,4,128,128]{4,3,2,1,0:T(8,128)} %param.7) | copy-start | bytes 4718596
  115.4 416.4 %all-to-all-start = ((f32[16,128,512]{2,1,0:T(8,128)}), f32[16,128,512]{2,1,0:T(8,128)}, u32[]{:S(2)}, u32[]{:S(2)}) async-start(f32[16,128,512]{2,1,0:T(8,128)} %stack.6), calls=%async_computation | async-start | bytes 8388608 | tf_op jit(solution)/shard_map/all_to_all | solution.py:42
  120.1 404.9 %all-reduce.3.cloned.1.call-start = ((), (), s32[]{:S(2)}) async-start(), calls=%async_computation.2 | async-start | bytes 6291456 | tf_op jit(solution)/shard_map/psum | solution.py:9
  124.3 0.7 copy-start.4
  124.3 0.7 copy-start.3
  531.8 5.9 %copy-start.1 = (f32[6,4,128,128]{3,2,1,0:T(8,128)S(1)}, f32[6,4,128,128]{3,2,1,0:T(8,128)}, u32[]{:S(2)}) copy-start(f32[6,4,128,128]{3,2,1,0:T(8,128)} %get-tuple-element.7) | copy-start | bytes 4718596
Sparse Core Ops, SparseCore 0:
  124.4 400.5 all-reduce.2
